TPU v7x, 256 devices: a whole 4x4x8 slice. The times are simulated.
256 devices in a mesh: dp: 16 (over x_lo, z), tensor: 16 (over x_hi, y, core).
Axes of the slice: x: 4 (x_hi: 2, x_lo: 2; x = x_hi * 2 + x_lo), y: 4, z: 8, core: 2. Of those that a mesh axis runs over, the one named last changes fastest.
Arguments:
- hidden: bfloat16 [4096, 8192], P('dp', 'tensor'), may hold values from -6 to 6
- connector: bfloat16 [8192, 3584], P('tensor'), may hold values from -0.0625 to 0.0625
- routing: int32 [4096, 1], P('dp'), may hold values from 0 to 15; in each aligned block of 256 rows (0 to 255, 256 to 511, ...) at most 32 rows name the same one
- talker_in: bfloat16 [8192, 3584], P(('dp', 'tensor')), may hold values from -6 to 6
- norm_gain: float32 [3584], replicated, may hold values from 0.25 to 1.75
- kv_weight: bfloat16 [3584, 1024], replicated, may hold values from -0.09375 to 0.09375
- kv_grad: bfloat16 [8192, 1024], P(('dp', 'tensor')), may hold values from -24 to 24
Outputs:
- hidden_grad: bfloat16 [4096, 8192], P('dp', 'tensor')
- connector_grad: float32 [8192, 3584], P('tensor', 'dp')
- kv_weight_grad: float32 [3584, 1024], P(None, ('dp', 'tensor'))
Inputs may be any that keep to these rules, and one draw needn't show every extreme that they name: `routing`: among the 256 rows of one index of dp, at most 32 go to one shard.
All inputs are finite; a program needn't handle non-finite values.
Results may differ from a plain program's by a relative error of at most 0.005.
Values may be sent and summed in bfloat16 or wider, within the bound.
A program may use at most 64 MiB of HBM per device.

v0:
```python
import math
import jax
import jax.numpy as jnp
from jax import lax
from jax.sharding import Mesh
from jax.sharding import PartitionSpec as P

TENSOR = ("tensor_0", "tensor_1", "tensor_2")
DP_TENSOR = ("dp", "tensor_0", "tensor_1", "tensor_2")
CONTRACT_LAST = (((1,), (1,)), ((), ()))
CONTRACT_FIRST = (((0,), (0,)), ((), ()))


def cut_along(value, dim, size):
    before, after = (value.shape[:dim], value.shape[dim + 1 :])
    return jnp.moveaxis(value.reshape(*before, size, -1, *after), dim, 0)


def sum_at_owner(value, axis, dim):
    size = lax.axis_size(axis)
    pieces = lax.all_to_all(cut_along(value, dim, size), axis, 0, 0, tiled=True)
    return jnp.sum(pieces, axis=0)


def sent_to_all(value, axis):
    copies = jnp.broadcast_to(value, (lax.axis_size(axis), *value.shape))
    return lax.all_to_all(copies, axis, split_axis=0, concat_axis=0, tiled=True)


def in_order(pieces, dim):
    dims = list(pieces.shape[1:])
    dims[dim] *= pieces.shape[0]
    return jnp.moveaxis(pieces, 0, dim).reshape(dims)


def gather_axes(value, axes, dim):
    far, near = axes
    pieces = sent_to_all(sent_to_all(value, far), near)
    return in_order(pieces.swapaxes(0, 1).reshape(-1, *value.shape), dim)


def on_device(hidden, connector, routing, talker_in, norm_gain, kv_weight, kv_grad):
    dp_count = lax.axis_size("dp")
    tensor_count = lax.axis_size(TENSOR)
    rows_dev = hidden.shape[0]
    capacity = talker_in.shape[0]
    factor = 1.0 / math.sqrt(rows_dev * dp_count)
    route_rows = routing[:, 0]
    shards = jnp.arange(tensor_count, dtype=jnp.int32)
    onehot = (route_rows[:, None] == shards[None, :]).astype(jnp.int32)
    ranks = jnp.sum((jnp.cumsum(onehot, axis=0) - 1) * onehot, axis=1)
    slot_ids = route_rows * capacity + ranks
    counts = jnp.sum(onehot, axis=0)
    tensor_pos = lax.axis_index(TENSOR)
    own_count = jnp.sum(jnp.where(shards == tensor_pos, counts, 0))
    usable = jnp.arange(capacity, dtype=jnp.int32) < own_count
    masked = jnp.where(usable[:, None], kv_grad, jnp.zeros_like(kv_grad))
    inputs = talker_in.astype(jnp.float32)
    inv_rms = lax.rsqrt(jnp.mean(inputs * inputs, axis=1, keepdims=True) + 1e-06)
    scaled = inputs * inv_rms
    normed = (scaled * norm_gain).astype(jnp.bfloat16)
    back_grad = lax.dot_general(
        masked, kv_weight, CONTRACT_LAST, preferred_element_type=jnp.float32
    )
    gain_back = norm_gain * back_grad
    talker_grad = (
        inv_rms * (gain_back - scaled * jnp.mean(gain_back * scaled, axis=1, keepdims=True))
    ).astype(jnp.bfloat16)
    col_count = masked.shape[1]
    per_dev = col_count // (dp_count * tensor_count)
    group_rows = lax.all_gather(normed, TENSOR, axis=0, tiled=True)
    regrouped = masked.reshape(capacity, dp_count, tensor_count, per_dev)
    regrouped = regrouped.transpose(0, 2, 1, 3).reshape(capacity, col_count)
    group_cols = lax.all_to_all(regrouped, TENSOR, split_axis=1, concat_axis=0, tiled=True)
    block_terms = (
        lax.dot_general(group_rows, group_cols, CONTRACT_FIRST, preferred_element_type=jnp.float32)
        * factor
    )
    kv_weight_grad = sum_at_owner(block_terms, "dp", 1)
    gathered = gather_axes(talker_grad, (("tensor_0", "tensor_1"), "tensor_2"), 0)
    row_grad = jnp.take(gathered, slot_ids, axis=0)
    hidden_grad = lax.dot_general(
        row_grad, connector, CONTRACT_LAST, preferred_element_type=jnp.float32
    ).astype(jnp.bfloat16)
    conn_terms = (
        lax.dot_general(hidden, row_grad, CONTRACT_FIRST, preferred_element_type=jnp.float32)
        * factor
    )
    connector_grad = lax.psum_scatter(conn_terms, "dp", scatter_dimension=1, tiled=True)
    return (hidden_grad, connector_grad, kv_weight_grad)


def solution(mesh):
    finer = Mesh(
        mesh.devices.reshape(mesh.shape["dp"], 2, 4, 2), ("dp", "tensor_0", "tensor_1", "tensor_2")
    )
    return jax.shard_map(
        on_device,
        mesh=finer,
        in_specs=(
            P("dp", TENSOR),
            P(TENSOR, None),
            P("dp", None),
            P(DP_TENSOR, None),
            P(),
            P(),
            P(DP_TENSOR, None),
        ),
        out_specs=(P("dp", TENSOR), P(TENSOR, "dp"), P(None, DP_TENSOR)),
        check_vma=False,
    )
```

profile of v0, /device:TPU:8, one launch (start us, length us, event | category | flops | bytes accessed | tf_op | source)
XLA Modules:
  0.0 196.0 jit_solution(6129102235819686993)
XLA Ops:
  8.0 0.0 copy-start
  8.0 0.0 all-gather.2.cloned.1.call-start
  8.1 1.1 fusion.8
  9.2 0.7 fusion.11
  9.9 0.6 reduce-window.6
  10.5 0.2 slice_reduce_fusion
  10.7 0.9 fusion.10
  11.6 0.6 fusion.12
  12.2 0.6 iota_compare_fusion.2
  12.9 1.0 copy.15
  13.9 0.0 copy-start.1
  13.9 0.0 copy-start.2
  13.9 5.6 %fusion.3 = (f32[32]{0:T(128)S(1)}, f32[32,3584]{1,0:T(8,128)S(1)}) fusion(bf16[32,3584]{1,0:T(8,128)(2,1)} %param.10, f32[32]{0:T(128)S(1)} %add_rsqrt_fusion, bf16[32,1024]{0,1:T(8,128)(2,1)S(1)} %broadcast_select_fusion.3, bf16[3584,1024]{1,0:T(8,128)(2,1)} %param.12, f32[3584]{0:T(1024)} %param.11), kind=kOutput, calls=%fused_computation.11 | convolution fusion | flops 235454432 | bytes 8108288 | tf_op jit(solution)/shard_map/dot_general | solution.py:62
  19.5 0.0 copy-start.3
  19.6 0.0 copy-done.1
  19.6 0.0 copy-done.2
  19.6 0.9 fusion.7
  20.4 0.0 all-gather.2.cloned.1.call-update
  20.5 1.4 broadcast_in_dim.41
  21.9 7.4 %all-to-all-start = ((bf16[8,32,3584]{2,1,0:T(8,128)(2,1)}), bf16[8,32,3584]{2,1,0:T(8,128)(2,1)S(1)}, u32[]{:S(2)}, u32[]{:S(2)}) async-start(bf16[8,32,3584]{2,1,0:T(8,128)(2,1)} %broadcast_in_dim.41), calls=%async_computation | async-start | bytes 3670016 | tf_op jit(solution)/shard_map/all_to_all | solution.py:27
  29.2 0.0 reduce-scatter.2.cloned.1.call-start
  29.2 0.0 copy-done.3
  29.3 25.4 %all-to-all-done = bf16[8,32,3584]{2,1,0:T(8,128)(2,1)S(1)} async-done(((bf16[8,32,3584]{2,1,0:T(8,128)(2,1)}), bf16[8,32,3584]{2,1,0:T(8,128)(2,1)S(1)}, u32[]{:S(2)}, u32[]{:S(2)}) %all-to-all-start) | async-done | bytes 1835040 | tf_op jit(solution)/shard_map/all_to_all | solution.py:27
  54.7 0.4 broadcast_in_dim.42
  55.1 6.7 %all_to_all.34 = bf16[2,8,32,3584]{3,2,1,0:T(8,128)(2,1)S(1)} all-to-all(bf16[2,8,32,3584]{3,2,1,0:T(8,128)(2,1)S(1)} %broadcast_in_dim.42), channel_id=1, replica_groups=mesh['dp'=16,'tensor_0'=2,'tensor_1'=4,'tensor_2'=2] {'tensor_2'}, dimensions={0} | all-to-all | bytes 7340032 | tf_op jit(solution)/shard_map/all_to_all | solution.py:27
  61.7 2.0 %copy.16 = bf16[8,2,32,3584]{3,2,1,0:T(8,128)(2,1)} copy(bf16[8,2,32,3584]{3,2,0,1:T(8,128)(2,1)S(1)} %bitcast.42) | data formatting | bytes 7340032 | tf_op jit(solution)/shard_map/transpose | solution.py:39
  63.8 6.0 %gather_fusion = bf16[256,3584]{1,0:T(8,128)(2,1)S(1)} fusion(bf16[512,3584]{1,0:T(8,128)(2,1)} %bitcast.41, s32[1024]{0:T(1024)S(1)} %pad_clamp_fusion), kind=kCustom, calls=%fused_computation | custom fusion | bytes 3671040 | tf_op jit(solution)/shard_map/jit(_take)/gather | solution.py:81
  69.8 0.0 copy-done
  69.8 4.2 %multiply_bitcast_fusion = f32[512,3584]{0,1:T(8,128)} fusion(bf16[256,512]{1,0:T(8,128)(2,1)S(1)} %copy-done, bf16[256,3584]{1,0:T(8,128)(2,1)S(1)} %gather_fusion, pred[256]{0:T(512)(128)(4,1)S(1)} %get-tuple-element.5), kind=kOutput, calls=%fused_computation.1 | convolution fusion | flops 942276608 | bytes 9437440 | tf_op jit(solution)/shard_map/dot_general | solution.py:86
  74.1 0.0 reduce-scatter.2.cloned.1.call-update
  74.1 0.3 copy.18
  74.4 0.1 reshape.71
  74.5 12.2 %all_to_all.35 = bf16[16,2,1024]{2,1,0:T(2,128)(2,1)S(1)} all-to-all(bf16[16,2,1024]{2,1,0:T(2,128)(2,1)S(1)} %reshape.71), channel_id=1, replica_groups=mesh['dp'=16,'tensor_0'=2,'tensor_1'=4,'tensor_2'=2] {'tensor_0','tensor..., dimensions={0} | all-to-all | bytes 131072 | tf_op jit(solution)/shard_map/all_to_all | solution.py:74
  86.7 0.1 reshape.72
  86.9 4.4 %all-gather.2.cloned.1.call-done = bf16[512,3584]{1,0:T(8,128)(2,1)} async-done(((bf16[32,3584]{1,0:T(8,128)(2,1)}), bf16[512,3584]{1,0:T(8,128)(2,1)}) %all-gather.2.cloned.1.call-update) | async-done | bytes 3670032 | tf_op jit(solution)/shard_map/all_gather | solution.py:71
  91.3 2.8 %convolution_multiply_fusion = f32[3584,64]{0,1:T(8,128)S(1)} fusion(bf16[512,3584]{1,0:T(8,128)(2,1)} %all-gather.2.cloned.1.call-done, bf16[512,64]{1,0:T(8,128)(2,1)S(1)} %bitcast.46), kind=kOutput, calls=%fused_computation.2 | convolution fusion | flops 235110400 | bytes 4653056 | tf_op jit(solution)/shard_map/dot_general | solution.py:76
  94.1 1.2 reshape.60
  95.3 7.2 %all-to-all-start.3 = ((f32[16,3584,4]{1,2,0:T(4,128)}), f32[16,3584,4]{1,2,0:T(4,128)S(1)}, u32[]{:S(2)}, u32[]{:S(2)}) async-start(f32[16,3584,4]{1,2,0:T(4,128)} %bitcast.43), calls=%async_computation.4 | async-start | bytes 1835008 | tf_op jit(solution)/shard_map/all_to_all | solution.py:21
  102.5 3.9 %convolution_convert_fusion = bf16[256,512]{1,0:T(8,128)(2,1)} fusion(bf16[512,3584]{1,0:T(8,128)(2,1)} %param.8, bf16[256,3584]{1,0:T(8,128)(2,1)S(1)} %gather_fusion, pred[256]{0:T(512)(128)(4,1)S(1)} %get-tuple-element.5), kind=kOutput, calls=%fused_computation.5 | convolution fusion | flops 940572672 | bytes 5767424 | tf_op jit(solution)/shard_map/dot_general | solution.py:82
  106.5 32.0 %all-to-all-done.3 = f32[16,3584,4]{1,2,0:T(4,128)S(1)} async-done(((f32[16,3584,4]{1,2,0:T(4,128)}), f32[16,3584,4]{1,2,0:T(4,128)S(1)}, u32[]{:S(2)}, u32[]{:S(2)}) %all-to-all-start.3) | async-done | bytes 917536 | tf_op jit(solution)/shard_map/all_to_all | solution.py:21
  138.4 0.8 reduce_sum.62
  139.2 49.3 %reduce-scatter.2.cloned.1.call-done = f32[512,224]{0,1:T(8,128)} async-done(((f32[512,3584]{0,1:T(8,128)}), f32[512,224]{0,1:T(8,128)}) %reduce-scatter.2.cloned.1.call-update) | async-done | bytes 458768 | tf_op jit(solution)/shard_map/reduce_scatter | solution.py:89
  (8 shorter events, 0.2 us)
Async XLA Ops:
  8.0 61.8 %copy-start = (bf16[256,512]{1,0:T(8,128)(2,1)S(1)}, bf16[256,512]{1,0:T(8,128)(2,1)}, u32[]{:S(2)}) copy-start(bf16[256,512]{1,0:T(8,128)(2,1)} %param.7) | copy-start | bytes 786436
  8.0 83.2 %all-gather.2.cloned.1.call-start = ((), (), s32[]{:S(2)}) async-start(), calls=%async_computation.6 | async-start | bytes 3899392 | tf_op jit(solution)/shard_map/all_gather | solution.py:71
  13.9 5.6 %copy-start.1 = (bf16[32,3584]{1,0:T(8,128)(2,1)S(1)}, bf16[32,3584]{1,0:T(8,128)(2,1)}, u32[]{:S(2)}) copy-start(bf16[32,3584]{1,0:T(8,128)(2,1)} %param.10) | copy-start | bytes 688132
  13.9 5.6 %copy-start.2 = (f32[3584]{0:T(1024)S(1)}, f32[3584]{0:T(1024)}, u32[]{:S(2)}) copy-start(f32[3584]{0:T(1024)} %param.11) | copy-start | bytes 43012
  19.5 9.7 %copy-start.3 = (s32[256,1]{0,1:T(1,128)S(1)}, s32[256,1]{0,1:T(1,128)}, u32[]{:S(2)}) copy-start(s32[256,1]{0,1:T(1,128)} %param.9) | copy-start | bytes 3076
  21.9 32.8 %all-to-all-start = ((bf16[8,32,3584]{2,1,0:T(8,128)(2,1)}), bf16[8,32,3584]{2,1,0:T(8,128)(2,1)S(1)}, u32[]{:S(2)}, u32[]{:S(2)}) async-start(bf16[8,32,3584]{2,1,0:T(8,128)(2,1)} %broadcast_in_dim.41), calls=%async_computation | async-start | bytes 3670016 | tf_op jit(solution)/shard_map/all_to_all | solution.py:27
  29.2 159.3 %reduce-scatter.2.cloned.1.call-start = ((), (), s32[]{:S(2)}) async-start(), calls=%async_computation.5 | async-start | bytes 7798784 | tf_op jit(solution)/shard_map/reduce_scatter | solution.py:89
  95.3 43.1 %all-to-all-start.3 = ((f32[16,3584,4]{1,2,0:T(4,128)}), f32[16,3584,4]{1,2,0:T(4,128)S(1)}, u32[]{:S(2)}, u32[]{:S(2)}) async-start(f32[16,3584,4]{1,2,0:T(4,128)} %bitcast.43), calls=%async_computation.4 | async-start | bytes 1835008 | tf_op jit(solution)/shard_map/all_to_all | solution.py:21
Sparse Core Ops, SparseCore 0:
  20.6 70.6 all-gather.1
Sparse Core Ops, SparseCore 1:
  74.2 114.3 reduce-scatter.1
where the time goes:
time: 196 us
  waiting for transfers between devices  111 us (57%)
  blocking collectives  18.9 us (10%)
  matrix products  16.6 us (8%)
  between operations  15.6 us (8%)
  starting transfers between devices  14.7 us (8%)
  local copies, waits for them, and re-layouts  12.8 us (7%)
  other arithmetic  6.28 us (3%)
    reduce_scatter x1, waiting for transfers between devices, on_device(): lax.psum_scatter(conn_terms, 'dp', scatter_dimension=1, tiled=True)  49.3 us
    all_to_all x1, waiting for transfers between devices, sum_at_owner(): pieces = lax.all_to_all(cut_along(value, dim, size), axis, 0, 0, tiled=True)  32 us
    all_to_all x1, waiting for transfers between devices, sent_to_all(): return lax.all_to_all(copies, axis, split_axis=0, concat_axis=0, tiled=True)  25.4 us
    all_to_all x1, blocking collectives, on_device(): lax.all_to_all(regrouped, TENSOR, split_axis=1, concat_axis=0, tiled=True)  12.2 us
    all_to_all x1, starting transfers between devices, sent_to_all(): return lax.all_to_all(copies, axis, split_axis=0, concat_axis=0, tiled=True)  7.38 us
    all_to_all x1, starting transfers between devices, sum_at_owner(): pieces = lax.all_to_all(cut_along(value, dim, size), axis, 0, 0, tiled=True)  7.24 us
    all_to_all x1, blocking collectives, sent_to_all(): return lax.all_to_all(copies, axis, split_axis=0, concat_axis=0, tiled=True)  6.68 us
    gather x1, local copies, waits for them, and re-layouts, on_device(): row_grad = jnp.take(gathered, slot_ids, axis=0)  6.04 us
  transfers between devices with their start and end apart: 4, of which 4 were waited for; matrix products, arithmetic and copies ran while one was open for 12% of the time, Pallas kernels for 0%

commit v1 on v0

--- a/solution.py
+++ b/solution.py
@@ -68,7 +68,9 @@
     ).astype(jnp.bfloat16)
     col_count = masked.shape[1]
     per_dev = col_count // (dp_count * tensor_count)
-    group_rows = lax.all_gather(normed, TENSOR, axis=0, tiled=True)
+    group_rows = jnp.concatenate(
+        lax.all_to_all(jnp.stack([normed] * lax.axis_size(TENSOR)), TENSOR, 0, 0), axis=0
+    )
     regrouped = masked.reshape(capacity, dp_count, tensor_count, per_dev)
     regrouped = regrouped.transpose(0, 2, 1, 3).reshape(capacity, col_count)
     group_cols = lax.all_to_all(regrouped, TENSOR, split_axis=1, concat_axis=0, tiled=True)

time: 196 us -> 251 us (1.28); the launches traced: 196 us -> 247 us
  waiting for transfers between devices: 111 us -> 161 us
    all_to_all x0 -> x1, waiting for transfers between devices: none -> 117 us  [on_device(): lax.all_to_all(jnp.stack([normed] * lax.axis_size(TENSOR)), TENSOR, 0, 0)]
    reduce_scatter x1, waiting for transfers between devices: 49.3 us -> 0.01 us  [on_device(): lax.psum_scatter(conn_terms, 'dp', scatter_dimension=1, tiled=True)]
    all_to_all x1, waiting for transfers between devices: 32 us -> 21 us  [sum_at_owner(): pieces = lax.all_to_all(cut_along(value, dim, size), axis, 0, 0, tiled=True)]
    all_to_all x0 -> x1, starting transfers between devices: none -> 5.75 us  [on_device(): lax.all_to_all(jnp.stack([normed] * lax.axis_size(TENSOR)), TENSOR, 0, 0)]
    all_gather x1 -> x0, waiting for transfers between devices: 4.37 us -> none  [on_device(): group_rows = lax.all_gather(normed, TENSOR, axis=0, tiled=True)]
    all_to_all x1, starting transfers between devices: 7.24 us -> 3.63 us  [sum_at_owner(): pieces = lax.all_to_all(cut_along(value, dim, size), axis, 0, 0, tiled=True)]
  transfers between devices with their start and end apart: 4 -> 4, of which waited for: 4 -> 3; matrix products, arithmetic and copies ran while one was open for 12% -> 5% of each run, Pallas kernels for 0% -> 0%
where the time goes in v1:
time: 251 us; the launch traced here: 247 us
  waiting for transfers between devices  161 us (64%)
  blocking collectives  18.1 us (7%)
  starting transfers between devices  16.8 us (7%)
  matrix products  16.5 us (7%)
  local copies, waits for them, and re-layouts  15.1 us (6%)
  between operations  14.2 us (6%)
  other arithmetic  5.6 us (2%)
    all_to_all x1, waiting for transfers between devices, on_device(): lax.all_to_all(jnp.stack([normed] * lax.axis_size(TENSOR)), TENSOR, 0, 0)  117 us
    all_to_all x1, waiting for transfers between devices, sent_to_all(): return lax.all_to_all(copies, axis, split_axis=0, concat_axis=0, tiled=True)  23 us
    all_to_all x1, waiting for transfers between devices, sum_at_owner(): pieces = lax.all_to_all(cut_along(value, dim, size), axis, 0, 0, tiled=True)  21 us
    all_to_all x1, blocking collectives, on_device(): lax.all_to_all(regrouped, TENSOR, split_axis=1, concat_axis=0, tiled=True)  11.4 us
    all_to_all x1, starting transfers between devices, sent_to_all(): return lax.all_to_all(copies, axis, split_axis=0, concat_axis=0, tiled=True)  7.38 us
    all_to_all x1, blocking collectives, sent_to_all(): return lax.all_to_all(copies, axis, split_axis=0, concat_axis=0, tiled=True)  6.68 us
    gather x1, local copies, waits for them, and re-layouts, on_device(): row_grad = jnp.take(gathered, slot_ids, axis=0)  6.04 us
    all_to_all x1, starting transfers between devices, on_device(): lax.all_to_all(jnp.stack([normed] * lax.axis_size(TENSOR)), TENSOR, 0, 0)  5.75 us
  transfers between devices with their start and end apart: 4, of which 3 were waited for; matrix products, arithmetic and copies ran while one was open for 5% of the time, Pallas kernels for 0%

profile of v1, /device:TPU:8, one launch (start us, length us, event | category | flops | bytes accessed | tf_op | source)
XLA Modules:
  0.0 247.0 jit_solution(3805454367581694800)
XLA Ops:
  7.2 0.0 copy-start
  7.2 1.1 fusion.9
  8.3 0.7 fusion.13
  9.0 0.6 reduce-window.6
  9.6 0.2 slice_reduce_fusion
  9.8 0.9 fusion.12
  10.7 0.6 fusion.14
  11.3 0.6 iota_compare_fusion.2
  12.0 1.0 copy.16
  13.0 0.0 copy-start.1
  13.0 0.0 copy-start.2
  13.1 5.6 %fusion.4 = (f32[32]{0:T(128)S(1)}, f32[32,3584]{1,0:T(8,128)S(1)}) fusion(bf16[32,3584]{1,0:T(8,128)(2,1)} %param.10, f32[32]{0:T(128)S(1)} %add_rsqrt_fusion, bf16[32,1024]{0,1:T(8,128)(2,1)S(1)} %broadcast_select_fusion.3, bf16[3584,1024]{1,0:T(8,128)(2,1)} %param.12, f32[3584]{0:T(1024)} %param.11), kind=kOutput, calls=%fused_computation.12 | convolution fusion | flops 235454432 | bytes 8108288 | tf_op jit(solution)/shard_map/dot_general | solution.py:62
  18.7 0.0 copy-start.3
  18.7 0.0 copy-done.1
  18.7 0.0 copy-done.2
  18.7 0.2 fusion.8
  18.9 1.4 broadcast_in_dim.41
  20.3 7.4 %all-to-all-start = ((bf16[8,32,3584]{2,1,0:T(8,128)(2,1)}), bf16[8,32,3584]{2,1,0:T(8,128)(2,1)S(1)}, u32[]{:S(2)}, u32[]{:S(2)}) async-start(bf16[8,32,3584]{2,1,0:T(8,128)(2,1)} %broadcast_in_dim.41), calls=%async_computation | async-start | bytes 3670016 | tf_op jit(solution)/shard_map/all_to_all | solution.py:27
  27.7 0.0 reduce-scatter.2.cloned.1.call-start
  27.7 0.0 copy-done.3
  27.7 23.0 %all-to-all-done = bf16[8,32,3584]{2,1,0:T(8,128)(2,1)S(1)} async-done(((bf16[8,32,3584]{2,1,0:T(8,128)(2,1)}), bf16[8,32,3584]{2,1,0:T(8,128)(2,1)S(1)}, u32[]{:S(2)}, u32[]{:S(2)}) %all-to-all-start) | async-done | bytes 1835040 | tf_op jit(solution)/shard_map/all_to_all | solution.py:27
  50.7 0.4 broadcast_in_dim.42
  51.0 6.7 %all_to_all.36 = bf16[2,8,32,3584]{3,2,1,0:T(8,128)(2,1)S(1)} all-to-all(bf16[2,8,32,3584]{3,2,1,0:T(8,128)(2,1)S(1)} %broadcast_in_dim.42), channel_id=1, replica_groups=mesh['dp'=16,'tensor_0'=2,'tensor_1'=4,'tensor_2'=2] {'tensor_2'}, dimensions={0} | all-to-all | bytes 7340032 | tf_op jit(solution)/shard_map/all_to_all | solution.py:27
  57.7 2.0 copy.17
  59.7 6.0 %gather_fusion = bf16[256,3584]{1,0:T(8,128)(2,1)S(1)} fusion(bf16[512,3584]{1,0:T(8,128)(2,1)} %bitcast.48, s32[1024]{0:T(1024)S(1)} %pad_clamp_fusion), kind=kCustom, calls=%fused_computation | custom fusion | bytes 3671040 | tf_op jit(solution)/shard_map/jit(_take)/gather | solution.py:83
  65.8 0.0 copy-done
  65.8 4.2 %multiply_bitcast_fusion = f32[512,3584]{0,1:T(8,128)} fusion(bf16[256,512]{1,0:T(8,128)(2,1)S(1)} %copy-done, bf16[256,3584]{1,0:T(8,128)(2,1)S(1)} %gather_fusion, pred[256]{0:T(512)(128)(4,1)S(1)} %get-tuple-element.5), kind=kOutput, calls=%fused_computation.1 | convolution fusion | flops 942276608 | bytes 9437440 | tf_op jit(solution)/shard_map/dot_general | solution.py:88
  70.0 0.0 reduce-scatter.2.cloned.1.call-update
  70.1 0.3 copy.19
  70.4 0.1 reshape.75
  70.5 11.4 %all_to_all.37 = bf16[16,2,1024]{2,1,0:T(2,128)(2,1)S(1)} all-to-all(bf16[16,2,1024]{2,1,0:T(2,128)(2,1)S(1)} %reshape.75), channel_id=1, replica_groups=mesh['dp'=16,'tensor_0'=2,'tensor_1'=4,'tensor_2'=2] {'tensor_0','tensor..., dimensions={0} | all-to-all | bytes 131072 | tf_op jit(solution)/shard_map/all_to_all | solution.py:76
  81.9 2.3 stack.2
  84.2 5.8 %all-to-all-start.2 = ((bf16[16,32,3584]{2,1,0:T(8,128)(2,1)}), bf16[16,32,3584]{2,1,0:T(8,128)(2,1)}, u32[]{:S(2)}, u32[]{:S(2)}) async-start(bf16[16,32,3584]{2,1,0:T(8,128)(2,1)} %stack.2), calls=%async_computation.3 | async-start | bytes 7340032 | tf_op jit(solution)/shard_map/all_to_all | solution.py:72
  90.0 0.1 reshape.76
  90.1 116.8 %all-to-all-done.2 = bf16[16,32,3584]{2,1,0:T(8,128)(2,1)} async-done(((bf16[16,32,3584]{2,1,0:T(8,128)(2,1)}), bf16[16,32,3584]{2,1,0:T(8,128)(2,1)}, u32[]{:S(2)}, u32[]{:S(2)}) %all-to-all-start.2) | async-done | bytes 3670048 | tf_op jit(solution)/shard_map/all_to_all | solution.py:72
  206.9 2.8 %fusion = f32[3584,64]{0,1:T(8,128)S(1)} fusion(bf16[16,32,3584]{2,1,0:T(8,128)(2,1)} %all-to-all-done.2, bf16[16,32,64]{2,1,0:T(8,128)(2,1)S(1)} %reshape.76), kind=kOutput, calls=%fused_computation.3 | convolution fusion | flops 235110400 | bytes 4653056 | tf_op jit(solution)/shard_map/dot_general | solution.py:78
  209.7 1.2 reshape.63
  210.9 3.6 %all-to-all-start.4 = ((f32[16,3584,4]{1,2,0:T(4,128)}), f32[16,3584,4]{1,2,0:T(4,128)S(1)}, u32[]{:S(2)}, u32[]{:S(2)}) async-start(f32[16,3584,4]{1,2,0:T(4,128)} %bitcast.50), calls=%async_computation.5 | async-start | bytes 1835008 | tf_op jit(solution)/shard_map/all_to_all | solution.py:21
  214.6 3.9 %convolution_convert_fusion = bf16[256,512]{1,0:T(8,128)(2,1)} fusion(bf16[512,3584]{1,0:T(8,128)(2,1)} %param.8, bf16[256,3584]{1,0:T(8,128)(2,1)S(1)} %gather_fusion, pred[256]{0:T(512)(128)(4,1)S(1)} %get-tuple-element.5), kind=kOutput, calls=%fused_computation.6 | convolution fusion | flops 940572672 | bytes 5767424 | tf_op jit(solution)/shard_map/dot_general | solution.py:84
  218.4 21.0 %all-to-all-done.4 = f32[16,3584,4]{1,2,0:T(4,128)S(1)} async-done(((f32[16,3584,4]{1,2,0:T(4,128)}), f32[16,3584,4]{1,2,0:T(4,128)S(1)}, u32[]{:S(2)}, u32[]{:S(2)}) %all-to-all-start.4) | async-done | bytes 917536 | tf_op jit(solution)/shard_map/all_to_all | solution.py:21
  239.4 0.8 reduce_sum.62
  240.2 0.0 reduce-scatter.2.cloned.1.call-done
  (8 shorter events, 0.2 us)
Async XLA Ops:
  7.2 58.6 %copy-start = (bf16[256,512]{1,0:T(8,128)(2,1)S(1)}, bf16[256,512]{1,0:T(8,128)(2,1)}, u32[]{:S(2)}) copy-start(bf16[256,512]{1,0:T(8,128)(2,1)} %param.7) | copy-start | bytes 786436
  13.0 5.6 %copy-start.1 = (bf16[32,3584]{1,0:T(8,128)(2,1)S(1)}, bf16[32,3584]{1,0:T(8,128)(2,1)}, u32[]{:S(2)}) copy-start(bf16[32,3584]{1,0:T(8,128)(2,1)} %param.10) | copy-start | bytes 688132
  13.0 5.6 %copy-start.2 = (f32[3584]{0:T(1024)S(1)}, f32[3584]{0:T(1024)}, u32[]{:S(2)}) copy-start(f32[3584]{0:T(1024)} %param.11) | copy-start | bytes 43012
  18.7 9.0 %copy-start.3 = (s32[256,1]{0,1:T(1,128)S(1)}, s32[256,1]{0,1:T(1,128)}, u32[]{:S(2)}) copy-start(s32[256,1]{0,1:T(1,128)} %param.9) | copy-start | bytes 3076
  20.3 30.4 %all-to-all-start = ((bf16[8,32,3584]{2,1,0:T(8,128)(2,1)}), bf16[8,32,3584]{2,1,0:T(8,128)(2,1)S(1)}, u32[]{:S(2)}, u32[]{:S(2)}) async-start(bf16[8,32,3584]{2,1,0:T(8,128)(2,1)} %broadcast_in_dim.41), calls=%async_computation | async-start | bytes 3670016 | tf_op jit(solution)/shard_map/all_to_all | solution.py:27
  27.7 212.5 %reduce-scatter.2.cloned.1.call-start = ((), (), s32[]{:S(2)}) async-start(), calls=%async_computation.6 | async-start | bytes 7798784 | tf_op jit(solution)/shard_map/reduce_scatter | solution.py:91
  84.2 122.7 %all-to-all-start.2 = ((bf16[16,32,3584]{2,1,0:T(8,128)(2,1)}), bf16[16,32,3584]{2,1,0:T(8,128)(2,1)}, u32[]{:S(2)}, u32[]{:S(2)}) async-start(bf16[16,32,3584]{2,1,0:T(8,128)(2,1)} %stack.2), calls=%async_computation.3 | async-start | bytes 7340032 | tf_op jit(solution)/shard_map/all_to_all | solution.py:72
  210.9 28.5 %all-to-all-start.4 = ((f32[16,3584,4]{1,2,0:T(4,128)}), f32[16,3584,4]{1,2,0:T(4,128)S(1)}, u32[]{:S(2)}, u32[]{:S(2)}) async-start(f32[16,3584,4]{1,2,0:T(4,128)} %bitcast.50), calls=%async_computation.5 | async-start | bytes 1835008 | tf_op jit(solution)/shard_map/all_to_all | solution.py:21
Sparse Core Ops, SparseCore 0:
  70.2 93.5 reduce-scatter.1
